TPU v7x, 256 devices: a whole 4x4x8 slice. The times are simulated.
256 devices in a mesh: rep: 32 (over y, x, core), exp: 8 (over z).
Axes of the slice: x: 4, y: 4, z: 8, core: 2. Of those that a mesh axis runs over, the one named last changes fastest.
Arguments:
- tubelets: bfloat16 [32768, 1536], P(('rep', 'exp')), may hold values from -6 to 6
- embed_weight: bfloat16 [1536, 1024], replicated, may hold values from -0.15625 to 0.15625
- norm_gain: float32 [1024], replicated, may hold values from 0.1 to 1.9
- routes: int32 [32768, 2], P(('rep', 'exp')), may hold values from 0 to 63, all different within a row; in each aligned block of 128 rows (0 to 127, 128 to 255, ...) at most 6 rows name the same one
- gate_codes: int32 [32768, 2], P(('rep', 'exp')), may hold values from 0 to 8
- w_in: bfloat16 [64, 1024, 4096], P('exp', None, 'rep'), may hold values from -0.1875 to 0.1875
- w_down: bfloat16 [64, 1024, 4096], P('exp', None, 'rep'), may hold values from -0.09375 to 0.09375
Outputs:
- layer_out: bfloat16 [32768, 1024], P(('rep', 'exp'))
Inputs may be any that keep to these rules, and one draw needn't show every extreme that they name: Within each device's aligned block of 128 tokens no expert is named by more than 6 routes, a bound that some block reaches; a token's two experts differ.
All inputs are finite; a program needn't handle non-finite values.
Results may differ from a plain program's by a relative error of at most 0.012.
Values may be sent and summed in bfloat16 or wider, within the bound.
A program may use at most 128 MiB of HBM per device.

v0:
```python
import jax
import jax.numpy as jnp
from jax import lax
from jax.sharding import PartitionSpec as P


def swapped(array, axis, distance):
    return lax.ppermute(array, axis, [(i, i ^ 1 << distance) for i in range(lax.axis_size(axis))])


def layer_norm(values, norm_gain):
    floats = values.astype(jnp.float32)
    average = jnp.mean(floats, axis=-1, keepdims=True)
    centred = floats - average
    variance = jnp.mean(centred * centred, axis=-1, keepdims=True)
    return (centred * lax.rsqrt(variance + 1e-06) * norm_gain).astype(jnp.bfloat16)


def on_device(tubelets, embed_weight, norm_gain, routes, gate_codes, w_in, w_down):
    embedded = jnp.dot(tubelets, embed_weight, preferred_element_type=jnp.float32).astype(
        jnp.bfloat16
    )
    normed = layer_norm(embedded, norm_gain)
    tok_count = tubelets.shape[0]
    model_width = embedded.shape[1]
    local_experts = w_in.shape[0]
    experts_all = local_experts * lax.axis_size("exp")
    capacity = 3 * tok_count // experts_all
    flat_routes = routes.reshape(-1)
    onehot = (flat_routes[:, None] == jnp.arange(experts_all, dtype=jnp.int32)[None, :]).astype(
        jnp.int32
    )
    slot_rank = jnp.sum((jnp.cumsum(onehot, axis=0) - 1) * onehot, axis=1)
    target = flat_routes * capacity + slot_rank
    rows_rep = jnp.repeat(normed, 2, axis=0)
    buffer = jnp.zeros((experts_all * capacity, model_width), jnp.bfloat16).at[target].set(rows_rep)
    buffer = buffer.reshape(experts_all, capacity, model_width)
    arrived = lax.all_to_all(buffer, "exp", split_axis=0, concat_axis=1, tiled=True)
    group_bits = 3
    position = lax.axis_index("rep")
    rep_bits = lax.axis_size("rep").bit_length() - 1
    collected = arrived
    for bit in range(group_bits):
        partner = swapped(collected, "rep", bit)
        upper = position // (1 << bit) % 2 == 1
        collected = jnp.where(
            upper,
            jnp.concatenate([partner, collected], axis=1),
            jnp.concatenate([collected, partner], axis=1),
        )
    panels = jnp.stack([w_in, w_down], axis=0)
    for bit in range(group_bits, rep_bits):
        partner = swapped(panels, "rep", bit)
        upper = position // (1 << bit) % 2 == 1
        panels = jnp.where(
            upper,
            jnp.concatenate([partner, panels], axis=3),
            jnp.concatenate([panels, partner], axis=3),
        )
    hidden = jax.nn.gelu(
        jnp.einsum("erd,edf->erf", collected, panels[0], preferred_element_type=jnp.float32)
    ).astype(jnp.bfloat16)
    partial_out = jnp.einsum("erf,edf->erd", hidden, panels[1], preferred_element_type=jnp.float32)
    for bit in range(group_bits - 1, -1, -1):
        half_rows = partial_out.shape[1] // 2
        lower_half = partial_out[:, :half_rows]
        upper_half = partial_out[:, half_rows:]
        upper = position // (1 << bit) % 2 == 1
        keeping = jnp.where(upper, upper_half, lower_half)
        sending = jnp.where(upper, lower_half, upper_half)
        partial_out = keeping + swapped(sending, "rep", bit)
    expert_out = partial_out.astype(jnp.bfloat16)
    returned = lax.all_to_all(expert_out, "exp", split_axis=1, concat_axis=0, tiled=True)
    picked = returned.reshape(-1, model_width)[target].astype(jnp.float32)
    gate_vals = 0.25 + 0.125 * gate_codes.reshape(-1).astype(jnp.float32)
    combined = jnp.sum((picked * gate_vals[:, None]).reshape(tok_count, 2, model_width), axis=1)
    return (embedded.astype(jnp.float32) + combined).astype(jnp.bfloat16)


def solution(mesh):
    return jax.shard_map(
        on_device,
        mesh=mesh,
        in_specs=(
            P(("rep", "exp"), None),
            P(),
            P(),
            P(("rep", "exp"), None),
            P(("rep", "exp"), None),
            P("exp", None, "rep"),
            P("exp", None, "rep"),
        ),
        out_specs=P(("rep", "exp"), None),
        check_vma=False,
    )
```

profile of v0, /device:TPU:1, one launch (start us, length us, event | category | flops | bytes accessed | tf_op | source)
XLA Modules:
  0.0 605.1 jit_solution(3164134112343038408)
XLA Ops:
  0.0 4.7 pad_maximum_fusion
  10.6 85.7 %collective-permute-done.3 = bf16[2,8,1024,128]{3,2,1,0:T(8,128)(2,1)} collective-permute-done((bf16[2,8,1024,128]{3,2,1,0:T(8,128)(2,1)}, bf16[2,8,1024,128]{3,2,1,0:T(8,128)(2,1)}, u32[]{:S(2)}, u32[]{:S(2)}) %collective-permute-start.3) | collective-permute-done | bytes 4194336 | tf_op jit(solution)/shard_map/ppermute | solution.py:8
  96.3 7.8 %maximum_select_fusion.1 = bf16[2,8,1024,256]{3,2,1,0:T(8,128)(2,1)} fusion(bf16[1,8,1024,128]{3,2,1,0:T(8,128)(2,1)S(1)} %bitcast.39, bf16[1,8,1024,128]{3,2,1,0:T(8,128)(2,1)S(1)} %bitcast.41, bf16[2,8,1024,128]{3,2,1,0:T(8,128)(2,1)} %collective-permute-done.3, pred[]{:T(512)S(6)} %eq.64), kind=kLoop, calls=%fused_computation.8 | loop fusion | flops 54525952 | bytes 16777216 | tf_op jit(solution)/shard_map/jit(_where)/select_n | solution.py:55
  104.1 4.0 collective-permute-start.4
  111.5 33.9 %all_to_all.33 = bf16[64,6,1024]{2,1,0:T(8,128)(2,1)S(1)} all-to-all(bf16[64,6,1024]{2,1,0:T(8,128)(2,1)S(1)} %reshape.89), channel_id=1, replica_groups=mesh['rep'=32,'exp'=8] {'exp'}, dimensions={0} | all-to-all | bytes 1572864 | tf_op jit(solution)/shard_map/all_to_all | solution.py:38
  145.8 3.9 collective-permute-start
  153.2 34.5 %collective-permute-done.1 = bf16[8,96,1024]{2,0,1:T(8,128)(2,1)} collective-permute-done((bf16[8,96,1024]{2,0,1:T(8,128)(2,1)S(1)}, bf16[8,96,1024]{2,0,1:T(8,128)(2,1)}, u32[]{:S(2)}, u32[]{:S(2)}) %collective-permute-start.1) | collective-permute-done | bytes 1572896 | tf_op jit(solution)/shard_map/ppermute | solution.py:8
  187.7 3.1 maximum_select_fusion.3
  190.8 3.0 collective-permute-start.2
  193.8 67.3 %collective-permute-done.2 = bf16[8,192,1024]{2,0,1:T(8,128)(2,1)} collective-permute-done((bf16[8,192,1024]{2,0,1:T(8,128)(2,1)S(1)}, bf16[8,192,1024]{2,0,1:T(8,128)(2,1)}, u32[]{:S(2)}, u32[]{:S(2)}) %collective-permute-start.2) | collective-permute-done | bytes 3145760 | tf_op jit(solution)/shard_map/ppermute | solution.py:8
  261.1 6.4 %maximum_select_fusion.2 = bf16[8,384,1024]{2,0,1:T(8,128)(2,1)} fusion(bf16[8,192,1024]{2,0,1:T(8,128)(2,1)S(1)} %maximum_select_fusion.3, bf16[8,192,1024]{2,0,1:T(8,128)(2,1)} %collective-permute-done.2, pred[]{:T(512)S(6)} %eq.54), kind=kLoop, calls=%fused_computation.17 | loop fusion | flops 9437184 | bytes 12582913 | tf_op jit(solution)/shard_map/jit(_where)/select_n | solution.py:46
  267.5 20.0 %collective-permute-done.4 = bf16[2,8,1024,256]{3,2,1,0:T(8,128)(2,1)} collective-permute-done((bf16[2,8,1024,256]{3,2,1,0:T(8,128)(2,1)}, bf16[2,8,1024,256]{3,2,1,0:T(8,128)(2,1)}, u32[]{:S(2)}, u32[]{:S(2)}) %collective-permute-start.4) | collective-permute-done | bytes 8388640 | tf_op jit(solution)/shard_map/ppermute | solution.py:8
  287.5 19.3 %maximum_select_fusion = bf16[2,8,1024,512]{3,2,1,0:T(8,128)(2,1)} fusion(bf16[2,8,1024,256]{3,2,1,0:T(8,128)(2,1)} %maximum_select_fusion.1, bf16[2,8,1024,256]{3,2,1,0:T(8,128)(2,1)} %collective-permute-done.4, pred[]{:T(512)S(6)} %eq.63), kind=kLoop, calls=%fused_computation.2 | loop fusion | flops 75497472 | bytes 33554432 | tf_op jit(solution)/shard_map/jit(_where)/select_n | solution.py:55
  306.9 21.5 %fusion = f32[8,384,1024]{2,1,0:T(8,128)} fusion(bf16[2,8,1024,512]{3,2,1,0:T(8,128)(2,1)} %maximum_select_fusion, bf16[8,384,1024]{2,0,1:T(8,128)(2,1)} %maximum_select_fusion.2), kind=kOutput, calls=%fused_computation.5 | convolution fusion | flops 6456606720 | bytes 35651584 | tf_op jit(solution)/shard_map/erf,edf->erd/dot_general | solution.py:63
  328.4 6.1 %slice_select_fusion = f32[8,192,1024]{2,1,0:T(8,128)S(1)} fusion(f32[8,384,1024]{2,1,0:T(8,128)} %fusion, pred[]{:T(512)S(6)} %eq.54), kind=kLoop, calls=%fused_computation.20 | loop fusion | flops 1572864 | bytes 18874368 | tf_op jit(solution)/shard_map/jit(_where)/select_n | solution.py:70
  334.4 3.0 collective-permute-start.5
  337.4 133.7 %collective-permute-done.5 = f32[8,192,1024]{2,1,0:T(8,128)} collective-permute-done((f32[8,192,1024]{2,1,0:T(8,128)S(1)}, f32[8,192,1024]{2,1,0:T(8,128)}, u32[]{:S(2)}, u32[]{:S(2)}) %collective-permute-start.5) | collective-permute-done | bytes 6291488 | tf_op jit(solution)/shard_map/ppermute | solution.py:8
  471.1 8.7 %select_add_fusion = f32[8,192,1024]{2,1,0:T(8,128)S(1)} fusion(f32[8,192,1024]{2,1,0:T(8,128)} %collective-permute-done.5, f32[8,384,1024]{2,1,0:T(8,128)} %fusion, pred[]{:T(512)S(6)} %eq.54), kind=kLoop, calls=%fused_computation.19 | loop fusion | flops 3145728 | bytes 25165824 | tf_op jit(solution)/shard_map/add | solution.py:71
  481.6 65.5 %collective-permute-done.6 = f32[8,96,1024]{2,1,0:T(8,128)S(1)} collective-permute-done((f32[8,96,1024]{2,1,0:T(8,128)S(1)}, f32[8,96,1024]{2,1,0:T(8,128)S(1)}, u32[]{:S(2)}, u32[]{:S(2)}) %collective-permute-start.6) | collective-permute-done | bytes 3145760 | tf_op jit(solution)/shard_map/ppermute | solution.py:8
  548.8 4.1 collective-permute-start.7
  552.9 3.0 collective-permute-done.7
  557.8 8.0 %all-to-all-start.1 = ((bf16[8,48,1024]{2,0,1:T(8,128)(2,1)}), bf16[8,48,1024]{2,0,1:T(8,128)(2,1)}, u32[]{:S(2)}, u32[]{:S(2)}) async-start(bf16[8,48,1024]{2,0,1:T(8,128)(2,1)} %copy.27), calls=%async_computation.1 | async-start | bytes 1572864 | tf_op jit(solution)/shard_map/all_to_all | solution.py:73
  565.9 23.5 %all-to-all-done.1 = bf16[8,48,1024]{2,0,1:T(8,128)(2,1)} async-done(((bf16[8,48,1024]{2,0,1:T(8,128)(2,1)}), bf16[8,48,1024]{2,0,1:T(8,128)(2,1)}, u32[]{:S(2)}, u32[]{:S(2)}) %all-to-all-start.1) | async-done | bytes 786464 | tf_op jit(solution)/shard_map/all_to_all | solution.py:73
  594.4 3.6 gather_fusion
  (59 shorter events, 30.5 us)
Async XLA Ops:
  0.0 7.7 %copy-start = (bf16[1536,1024]{1,0:T(8,128)(2,1)S(1)}, bf16[1536,1024]{1,0:T(8,128)(2,1)}, u32[]{:S(2)}) copy-start(bf16[1536,1024]{1,0:T(8,128)(2,1)} %param.8) | copy-start | bytes 9437188
  0.0 6.9 %copy-start.7 = (s32[128,2]{0,1:T(2,128)S(1)}, s32[128,2]{0,1:T(2,128)}, u32[]{:S(2)}) copy-start(s32[128,2]{0,1:T(2,128)} %param.10) | copy-start | bytes 3076
  0.0 10.4 %copy-start.6 = (f32[1024]{0:T(1024)S(1)}, f32[1024]{0:T(1024)}, u32[]{:S(2)}) copy-start(f32[1024]{0:T(1024)} %param.9) | copy-start | bytes 12292
  4.7 91.5 %collective-permute-start.3 = (bf16[2,8,1024,128]{3,2,1,0:T(8,128)(2,1)}, bf16[2,8,1024,128]{3,2,1,0:T(8,128)(2,1)}, u32[]{:S(2)}, u32[]{:S(2)}) collective-permute-start(bf16[2,8,1024,128]{3,2,1,0:T(8,128)(2,1)} %pad_maximum_fusion), channel_id=1, source_target_pairs={{0,64},{8,72},{16,80},{24,88},{32,96},{40,104},{48,112},{56,120},{... | collective-permute-start | bytes 12582920 | tf_op jit(solution)/shard_map/ppermute | solution.py:8
  7.7 88.5 %copy-start.3 = (bf16[8,1024,128]{2,1,0:T(8,128)(2,1)S(1)}, bf16[8,1024,128]{2,1,0:T(8,128)(2,1)}, u32[]{:S(2)}) copy-start(bf16[8,1024,128]{2,1,0:T(8,128)(2,1)} %param.13) | copy-start | bytes 6291460
  7.8 88.5 %copy-start.4 = (bf16[8,1024,128]{2,1,0:T(8,128)(2,1)S(1)}, bf16[8,1024,128]{2,1,0:T(8,128)(2,1)}, u32[]{:S(2)}) copy-start(bf16[8,1024,128]{2,1,0:T(8,128)(2,1)} %param.12) | copy-start | bytes 6291460
  9.6 0.8 copy-start.2
  104.1 183.4 %collective-permute-start.4 = (bf16[2,8,1024,256]{3,2,1,0:T(8,128)(2,1)}, bf16[2,8,1024,256]{3,2,1,0:T(8,128)(2,1)}, u32[]{:S(2)}, u32[]{:S(2)}) collective-permute-start(bf16[2,8,1024,256]{3,2,1,0:T(8,128)(2,1)} %maximum_select_fusion.1), channel_id=1, source_target_pairs={{0,128},{8,136},{16,144},{24,152},{32,160},{40,168},{48,176},{56,1... | collective-permute-start | bytes 25165832 | tf_op jit(solution)/shard_map/ppermute | solution.py:8
  145.8 5.8 collective-permute-start
  151.9 1.3 copy-start.5
  151.9 35.8 %collective-permute-start.1 = (bf16[8,96,1024]{2,0,1:T(8,128)(2,1)S(1)}, bf16[8,96,1024]{2,0,1:T(8,128)(2,1)}, u32[]{:S(2)}, u32[]{:S(2)}) collective-permute-start(bf16[8,96,1024]{2,0,1:T(8,128)(2,1)S(1)} %maximum_select_fusion.4), channel_id=1, source_target_pairs={{0,16},{8,24},{16,0},{24,8},{32,48},{40,56},{48,32},{56,40},{64,80... | collective-permute-start | bytes 4718600 | tf_op jit(solution)/shard_map/ppermute | solution.py:8
  190.8 70.3 %collective-permute-start.2 = (bf16[8,192,1024]{2,0,1:T(8,128)(2,1)S(1)}, bf16[8,192,1024]{2,0,1:T(8,128)(2,1)}, u32[]{:S(2)}, u32[]{:S(2)}) collective-permute-start(bf16[8,192,1024]{2,0,1:T(8,128)(2,1)S(1)} %maximum_select_fusion.3), channel_id=1, source_target_pairs={{0,32},{8,40},{16,48},{24,56},{32,0},{40,8},{48,16},{56,24},{64,96... | collective-permute-start | bytes 9437192 | tf_op jit(solution)/shard_map/ppermute | solution.py:8
  334.4 136.7 %collective-permute-start.5 = (f32[8,192,1024]{2,1,0:T(8,128)S(1)}, f32[8,192,1024]{2,1,0:T(8,128)}, u32[]{:S(2)}, u32[]{:S(2)}) collective-permute-start(f32[8,192,1024]{2,1,0:T(8,128)S(1)} %slice_select_fusion), channel_id=1, source_target_pairs={{0,32},{8,40},{16,48},{24,56},{32,0},{40,8},{48,16},{56,24},{64,96... | collective-permute-start | bytes 18874376 | tf_op jit(solution)/shard_map/ppermute | solution.py:8
  480.5 66.6 %collective-permute-start.6 = (f32[8,96,1024]{2,1,0:T(8,128)S(1)}, f32[8,96,1024]{2,1,0:T(8,128)S(1)}, u32[]{:S(2)}, u32[]{:S(2)}) collective-permute-start(f32[8,96,1024]{2,1,0:T(8,128)S(1)} %slice_select_fusion.1), channel_id=1, source_target_pairs={{0,16},{8,24},{16,0},{24,8},{32,48},{40,56},{48,32},{56,40},{64,80... | collective-permute-start | bytes 9437192 | tf_op jit(solution)/shard_map/ppermute | solution.py:8
  548.5 17.3 %copy-start.8 = (s32[128,2]{0,1:T(2,128)S(1)}, s32[128,2]{0,1:T(2,128)}, u32[]{:S(2)}) copy-start(s32[128,2]{0,1:T(2,128)} %param.11) | copy-start | bytes 3076
  548.8 7.1 %collective-permute-start.7 = (f32[8,48,1024]{2,1,0:T(8,128)S(1)}, f32[8,48,1024]{2,1,0:T(8,128)S(1)}, u32[]{:S(2)}, u32[]{:S(2)}) collective-permute-start(f32[8,48,1024]{2,1,0:T(8,128)S(1)} %slice_select_fusion.2), channel_id=1, source_target_pairs={{0,8},{8,0},{16,24},{24,16},{32,40},{40,32},{48,56},{56,48},{64,72... | collective-permute-start | bytes 4718600 | tf_op jit(solution)/shard_map/ppermute | solution.py:8
  557.8 31.7 %all-to-all-start.1 = ((bf16[8,48,1024]{2,0,1:T(8,128)(2,1)}), bf16[8,48,1024]{2,0,1:T(8,128)(2,1)}, u32[]{:S(2)}, u32[]{:S(2)}) async-start(bf16[8,48,1024]{2,0,1:T(8,128)(2,1)} %copy.27), calls=%async_computation.1 | async-start | bytes 1572864 | tf_op jit(solution)/shard_map/all_to_all | solution.py:73
  589.5 15.6 %copy-start.1 = (bf16[1536,1024]{1,0:T(8,128)(2,1)S(1)}, bf16[1536,1024]{1,0:T(8,128)(2,1)}, u32[]{:S(2)}) copy-start(bf16[1536,1024]{1,0:T(8,128)(2,1)} %param.8) | copy-start | bytes 9437188
where the time goes:
time: 606 us; the launch traced here: 605 us
  waiting for transfers between devices  435 us (72%)
  other arithmetic  64.9 us (11%)
  blocking collectives  33.9 us (6%)
  starting transfers between devices  30.4 us (5%)
  matrix products  23.3 us (4%)
  local copies, waits for them, and re-layouts  17.2 us (3%)
    ppermute x8, waiting for transfers between devices, swapped(): lax.ppermute(array, axis, [(i, i ^ 1 << distance) for i in range(lax.axis...  412 us
    all_to_all x1, blocking collectives, on_device(): lax.all_to_all(buffer, 'exp', split_axis=0, concat_axis=1, tiled=True)  33.9 us
    select_n x2, other arithmetic, on_device(): jnp.where(upper, jnp.concatenate([partner, panels], axis=3), jnp.concaten...  27.2 us
    all_to_all x1, waiting for transfers between devices, on_device(): lax.all_to_all(expert_out, 'exp', split_axis=1, concat_axis=0, tiled=True)  23.5 us
    ppermute x8, starting transfers between devices, swapped(): lax.ppermute(array, axis, [(i, i ^ 1 << distance) for i in range(lax.axis...  22.4 us
    dot_general x1, matrix products, on_device(): jnp.einsum('erf,edf->erd', hidden, panels[1], preferred_element_type=jnp....  21.5 us
  transfers between devices with their start and end apart: 9, of which 9 were waited for; matrix products, arithmetic and copies ran while one was open for 3% of the time, Pallas kernels for 0%

commit v1 on v0

v1 whole, which is shorter than its diff:
```python
import functools

import jax
import jax.numpy as jnp
from jax import lax
from jax.experimental import pallas as pl
from jax.experimental.pallas import tpu as pltpu
from jax.sharding import PartitionSpec as P

ORDER = (0, 1, 7, 2, 6, 3, 5, 4)
BF = jnp.bfloat16
F32 = jnp.float32


def kernel(
    tub_ref, emb_ref, gain_ref, routes_ref, codes_ref, win_ref, wdn_ref,
    out_ref,
    tub, emb, embedded, gate, disp, recv1, send2, xs, w1, w2, stage, part, own, acc, stage3, half2, back, ret1,
    send3, ret2,
    load_sem, wl_sem, ws_sem, wr_sem, fs_sem, fr_sem, as_sem, ar_sem, zs_sem, zr_sem, gs_sem, gr_sem,
    hs_sem, hr_sem, ps_sem, pr_sem, ys_sem, yr_sem, bs_sem, br_sem,
):
    r = lax.axis_index("rep")
    z = lax.axis_index("exp")
    c = r % 2
    x = (r // 2) % 4
    y = r // 8

    def at(px, py, core, pz=None):
        rep = ((py + 8) % 4 * 4 + (px + 8) % 4) * 2 + core
        return (rep, z if pz is None else pz)

    def line(kind, j, core):
        return at(x + (1 - kind) * j, y + kind * j, core)

    def copy(src, dst, ssem, rsem, dev):
        return pltpu.make_async_remote_copy(
            src_ref=src, dst_ref=dst, send_sem=ssem, recv_sem=rsem, device_id=dev, device_id_type=pl.DeviceIdType.MESH
        )

    loads = [
        pltpu.make_async_copy(tub_ref, tub, load_sem.at[0]),
        pltpu.make_async_copy(emb_ref, emb, load_sem.at[1]),
    ]
    for cp in loads:
        cp.start()

    barrier = pltpu.get_barrier_semaphore()
    peers = [line(kind, j, core) for kind in (0, 1) for j in (1, 2, 3) for core in (0, 1)]
    peers += [at(x, y, 1 - c)] + [(r, (z + d) % 8) for d in range(1, 8)]
    for dev in peers:
        pl.semaphore_signal(barrier, inc=1, device_id=dev, device_id_type=pl.DeviceIdType.MESH)

    own_k = c * 4 + x + c * (y - x)
    w_own = [
        pltpu.make_async_copy(win_ref.at[own_k], w1.at[:, 0:128], wl_sem.at[0]),
        pltpu.make_async_copy(wdn_ref.at[own_k], w2.at[:, 0:128], wl_sem.at[1]),
    ]
    for cp in w_own:
        cp.start()
    for cp in loads:
        cp.wait()

    e = jnp.dot(tub[...], emb[...], preferred_element_type=F32).astype(BF)
    embedded[...] = e
    ef = e.astype(F32)
    centred = ef - jnp.mean(ef, axis=-1, keepdims=True)
    var = jnp.mean(centred * centred, axis=-1, keepdims=True)
    normed = (centred * lax.rsqrt(var + 1e-06) * gain_ref[...]).astype(BF)

    experts = lax.broadcasted_iota(jnp.int32, (64, 128), 0)
    hot = [(experts == routes_ref[k : k + 1, :]).astype(F32) for k in (0, 1)]
    before = (
        lax.broadcasted_iota(jnp.int32, (128, 128), 0) < lax.broadcasted_iota(jnp.int32, (128, 128), 1)
    ).astype(F32).astype(BF)
    count = jnp.dot((hot[0] + hot[1]).astype(BF), before, preferred_element_type=F32)
    slots = lax.broadcasted_iota(jnp.int32, (384, 128), 0)
    picks = []
    for k in (0, 1):
        ex = routes_ref[k : k + 1, :]
        rank = jnp.sum(hot[k] * count, axis=0, keepdims=True).astype(jnp.int32)
        d = ((ex >> 3) - z) & 7
        place = jnp.where(d <= 4, jnp.maximum(2 * d - 1, 0), 16 - 2 * d)
        kind = (ex >> 2) & 1
        j = ((ex & 3) - (x + kind * (y - x))) & 3
        block = ((kind + c) & 1) * 4 + j
        picks.append(slots == block * 48 + place * 6 + rank)
    dispatch = (picks[0].astype(F32) + picks[1].astype(F32)).astype(BF)
    vals = [0.25 + 0.125 * codes_ref[k : k + 1, :].astype(F32) for k in (0, 1)]
    gate[...] = (picks[0].astype(F32) * vals[0] + picks[1].astype(F32) * vals[1]).astype(BF)
    rows = jnp.dot(dispatch, normed, preferred_element_type=F32).astype(BF).reshape(8, 48, 1024)
    disp[...] = rows
    recv1[0] = rows[0]
    pl.semaphore_wait(barrier, 20)

    sends = []
    a_copies = []
    for b in range(1, 8):
        j, other = b % 4, b // 4
        core = other + c - 2 * other * c
        cp = copy(disp.at[b], recv1.at[b], as_sem.at[b], ar_sem.at[b], line(core, j, core))
        cp.start()
        a_copies.append(cp)
    sends += a_copies

    w_copies = {}
    for b in (1, 5, 3, 7, 4, 2, 6):
        j, other = b % 4, b // 4
        core = other + c - 2 * other * c
        k = core * 4 + ((x + core * (y - x)) + j) % 4
        cols = pl.ds(b * 128, 128)
        for m, (src, dst) in enumerate(((win_ref, w1), (wdn_ref, w2))):
            if j == 2:
                step = 1 if m == 0 else 3
                cp = copy(
                    src.at[k], stage.at[m * 2 + other], ws_sem.at[b * 2 + m], fr_sem.at[m * 2 + other],
                    line(core, step, core),
                )
            else:
                cp = copy(
                    src.at[k], dst.at[:, cols], ws_sem.at[b * 2 + m], wr_sem.at[b * 2 + m], line(core, j, core)
                )
            cp.start()
            w_copies[b, m] = cp
            sends.append(cp)

    ri = lax.broadcasted_iota(jnp.int32, (384, 384), 0)
    ci = lax.broadcasted_iota(jnp.int32, (384, 384), 1)
    perm = (ci == (ri % 48) // 6 * 48 + ri // 48 * 6 + ri % 6).astype(F32).astype(BF)
    for cp in a_copies:
        cp.wait_recv()
    moved = jnp.dot(perm, recv1[...].reshape(384, 1024), preferred_element_type=F32).astype(BF).reshape(8, 48, 1024)
    send2[...] = moved
    xs[0, 0, 0:48] = moved[0]
    z_copies = [None]
    for p in range(1, 8):
        dst = xs.at[0, p // 2, pl.ds(p % 2 * 48, 48)]
        cp = copy(send2.at[p], dst, zs_sem.at[p], zr_sem.at[p], (r, (z + ORDER[p]) % 8))
        cp.start()
        z_copies.append(cp)
        sends.append(cp)

    def b_line(j):
        return line(1 - c, j, c)

    relays = []
    for m in (0, 1):
        for other in (0, 1):
            copy(
                win_ref.at[0], stage.at[m * 2 + other], fs_sem.at[m * 2 + other], fr_sem.at[m * 2 + other],
                line(c, 1, c),
            ).wait_recv()
            cols = pl.ds((2 + 4 * other) * 128, 128)
            cp = copy(
                stage.at[m * 2 + other], (w1, w2)[m].at[:, cols], fs_sem.at[m * 2 + other],
                wr_sem.at[(2 + 4 * other) * 2 + m], line(c, 1 if m == 0 else 3, c),
            )
            cp.start()
            relays.append(cp)
            sends.append(cp)
            w_copies[2 + 4 * other, m] = cp

    g_copies = {}
    for g in range(4):
        for p in (2 * g, 2 * g + 1):
            if p:
                z_copies[p].wait_recv()
        for j in (1, 3):
            cp = copy(xs.at[0, g], xs.at[j, g], gs_sem.at[g, j], gr_sem.at[g, j], b_line(j))
            cp.start()
            g_copies[g, j] = cp
            sends.append(cp)

    def forward(g):
        for j, i in ((1, 0), (3, 1)):
            g_copies[g, j].wait_recv()
            half = pl.ds(i * 48, 48)
            cp = copy(xs.at[j, g, half], xs.at[2, g, half], hs_sem.at[g, i], hr_sem.at[g, i], b_line(j))
            cp.start()
            g_copies[g, 4 + i] = cp
            sends.append(cp)

    for g in range(4):
        forward(g)

    for cp in w_own:
        cp.wait()
    for b in range(1, 8):
        for m in (0, 1):
            w_copies[b, m].wait_recv()

    h_copies, p_copies, y_copies = {}, {}, [None]

    def compute(g):
        g_copies[g, 4].wait_recv()
        g_copies[g, 5].wait_recv()
        block = xs[:, g].reshape(384, 1024)
        hidden = jnp.dot(block, w1[...], preferred_element_type=F32)
        hidden = jax.nn.gelu(hidden).astype(BF)
        res = lax.dot_general(hidden, w2[...], (((1,), (1,)), ((), ())), preferred_element_type=F32)
        res = res.reshape(4, 96, 1024)
        own[g] = res[0]
        for j in (2, 1, 3):
            part[j, g] = res[j].astype(BF)
        for i, j in ((0, 3), (1, 1)):
            cp = copy(
                part.at[2, g, pl.ds(i * 48, 48)], half2.at[i, g], ps_sem.at[g, i], pr_sem.at[g, i], b_line(j)
            )
            cp.start()
            h_copies[g, i] = cp
            sends.append(cp)

    def pass_on(g):
        for i, j in ((0, 1), (1, 3)):
            h_copies[g, i].wait_recv()
            half = pl.ds(i * 48, 48)
            part[j, g, half] = (part[j, g, half].astype(F32) + half2[i, g].astype(F32)).astype(BF)
            cp = copy(part.at[j, g], stage3.at[j // 2, g], ys_sem.at[g, i], yr_sem.at[g, i], b_line(4 - j))
            cp.start()
            p_copies[g, i] = cp
            sends.append(cp)

    def finish(g):
        p_copies[g, 0].wait_recv()
        p_copies[g, 1].wait_recv()
        total = own[g] + stage3[0, g].astype(F32) + stage3[1, g].astype(F32)
        total = total.astype(BF)
        back[g] = total
        if g == 0:
            ret1[0] = total[0:48]
        for p in (2 * g, 2 * g + 1):
            if p:
                cp = copy(
                    back.at[g, pl.ds(p % 2 * 48, 48)], ret1.at[p], bs_sem.at[p], br_sem.at[p],
                    (r, (z + 8 - ORDER[p]) % 8),
                )
                cp.start()
                y_copies.append(cp)
                sends.append(cp)

    compute(0)
    compute(1)
    pass_on(0)
    compute(2)
    finish(0)
    pass_on(1)
    compute(3)
    finish(1)
    pass_on(2)
    pass_on(3)
    finish(2)
    finish(3)

    for cp in y_copies[1:]:
        cp.wait_recv()
    moved = jnp.dot(perm, ret1[...].reshape(384, 1024), preferred_element_type=F32).astype(BF).reshape(8, 48, 1024)
    send3[...] = moved
    ret2[0] = moved[0]
    last = []
    for b in range(1, 8):
        j, other = b % 4, b // 4
        core = other + c - 2 * other * c
        cp = copy(send3.at[b], ret2.at[b], acc.at[b], acc.at[8 + b], line(c, 4 - j, core))
        cp.start()
        last.append(cp)
        sends.append(cp)
    for cp in last:
        cp.wait_recv()
    combined = lax.dot_general(
        gate[...], ret2[...].reshape(384, 1024), (((0,), (0,)), ((), ())), preferred_element_type=F32
    )
    out_ref[...] = (embedded[...].astype(F32) + combined).astype(BF)
    for cp in sends:
        cp.wait_send()


def on_device(tubelets, embed_weight, norm_gain, routes, gate_codes, w_in, w_down):
    dma = pltpu.SemaphoreType.DMA
    vmem = pltpu.VMEM
    anyspace = pl.BlockSpec(memory_space=pl.ANY)
    local = pl.BlockSpec(memory_space=pltpu.VMEM)
    return pl.pallas_call(
        kernel,
        out_shape=jax.ShapeDtypeStruct((128, 1024), BF),
        in_specs=[anyspace, anyspace, local, local, local, anyspace, anyspace],
        out_specs=local,
        scratch_shapes=[
            vmem((128, 1536), BF),
            vmem((1536, 1024), BF),
            vmem((128, 1024), BF),
            vmem((384, 128), BF),
            vmem((8, 48, 1024), BF),
            vmem((8, 48, 1024), BF),
            vmem((8, 48, 1024), BF),
            vmem((4, 4, 96, 1024), BF),
            vmem((1024, 1024), BF),
            vmem((1024, 1024), BF),
            vmem((4, 1024, 128), BF),
            vmem((4, 4, 96, 1024), BF),
            vmem((4, 96, 1024), F32),
            dma((16,)),
            vmem((2, 4, 96, 1024), BF),
            vmem((2, 4, 48, 1024), BF),
            vmem((4, 96, 1024), BF),
            vmem((8, 48, 1024), BF),
            vmem((8, 48, 1024), BF),
            vmem((8, 48, 1024), BF),
            dma((2,)),
            dma((2,)),
            dma((16,)),
            dma((16,)),
            dma((4,)),
            dma((4,)),
            dma((8,)),
            dma((8,)),
            dma((8,)),
            dma((8,)),
            dma((4, 4)),
            dma((4, 4)),
            dma((4, 2)),
            dma((4, 2)),
            dma((4, 2)),
            dma((4, 2)),
            dma((4, 2)),
            dma((4, 2)),
            dma((8,)),
            dma((8,)),
        ],
        compiler_params=pltpu.CompilerParams(
            collective_id=0, has_side_effects=True, vmem_limit_bytes=60 * 1024 * 1024
        ),
        name="moe_layer",
    )(tubelets, embed_weight, norm_gain.reshape(1, 1024), routes.T, gate_codes.T, w_in, w_down)


def solution(mesh):
    return jax.shard_map(
        on_device,
        mesh=mesh,
        in_specs=(
            P(("rep", "exp"), None),
            P(),
            P(),
            P(("rep", "exp"), None),
            P(("rep", "exp"), None),
            P("exp", None, "rep"),
            P("exp", None, "rep"),
        ),
        out_specs=P(("rep", "exp"), None),
        check_vma=False,
    )
```

time: 606 us -> 101 us (0.17)
  waiting for transfers between devices: 435 us -> 0 us
  Pallas kernels: 0 us -> 98.9 us
  other arithmetic: 64.9 us -> 0 us
  blocking collectives: 33.9 us -> 0 us
  starting transfers between devices: 30.4 us -> 0 us
  matrix products: 23.3 us -> 0 us
  local copies, waits for them, and re-layouts: 17.2 us -> 1.67 us
    ppermute x8 -> x0, waiting for transfers between devices: 412 us -> none  [swapped(): lax.ppermute(array, axis, [(i, i ^ 1 << distance) for i in range(lax.axis...]
    pallas_call x0 -> x1, Pallas kernels: none -> 98.9 us  [on_device(): pl.pallas_call(kernel, out_shape=jax.ShapeDtypeStruct((128, 1024), BF), i...]
    select_n x9 -> x0, other arithmetic: 44 us -> none  [the longest x2 27.2 us: on_device(): jnp.where(upper, jnp.concatenate([partner, panels], axis=3), jnp.concaten...]
    all_to_all x1 -> x0, blocking collectives: 33.9 us -> none  [on_device(): lax.all_to_all(buffer, 'exp', split_axis=0, concat_axis=1, tiled=True)]
    all_to_all x1 -> x0, waiting for transfers between devices: 23.5 us -> none  [on_device(): lax.all_to_all(expert_out, 'exp', split_axis=1, concat_axis=0, tiled=True)]
    dot_general x2 -> x0, matrix products: 23.3 us -> none  [the longest x1 21.5 us: on_device(): jnp.einsum('erf,edf->erd', hidden, panels[1], preferred_element_type=jnp....]
    ppermute x8 -> x0, starting transfers between devices: 22.4 us -> none  [swapped(): lax.ppermute(array, axis, [(i, i ^ 1 << distance) for i in range(lax.axis...]
    add x3 -> x0, other arithmetic: 10.1 us -> none  [the longest x2 10.1 us: on_device(): partial_out = keeping + swapped(sending, 'rep', bit)]
  transfers between devices with their start and end apart: 9 -> 0, of which waited for: 9 -> 0; matrix products, arithmetic and copies ran while one was open for 3% -> 0% of each run, Pallas kernels for 0% -> 0%
where the time goes in v1:
time: 101 us
  Pallas kernels  98.9 us (98%)
  local copies, waits for them, and re-layouts  1.67 us (2%)
    pallas_call x1, Pallas kernels, on_device(): pl.pallas_call(kernel, out_shape=jax.ShapeDtypeStruct((128, 1024), BF), i...  98.9 us

profile of v1, /device:TPU:1, one launch (start us, length us, event | category | flops | bytes accessed | tf_op | source)
XLA Modules:
  0.0 100.6 jit_solution(3612179470647635725)
XLA Ops:
  0.0 98.9 %moe_layer.1 = bf16[128,1024]{1,0:T(8,128)(2,1)} custom-call(bf16[128,1536]{1,0:T(8,128)(2,1)} %tub_ref.1, bf16[1536,1024]{1,0:T(8,128)(2,1)} %emb_ref.1, f32[1,1024]{1,0:T(1,128)} %bitcast.3, s32[2,128]{1,0:T(2,128)} %bitcast.4, s32[2,128]{1,0:T(2,128)} %bitcast.5, bf16[8,1024,128]{2,1,0:T(8,128)(2,1)} %win_ref.1, bf16[8,1024,128]{2,1,0:T(8,128)(2,1)} %wdn_ref.1), custom_call_target="tpu_custom_call" | custom-call | tf_op jit(solution)/shard_map/moe_layer/pallas_call | solution.py:282
  98.9 1.7 %copy.9 = bf16[128,1024]{1,0:T(8,128)(2,1)} copy(bf16[128,1024]{1,0:T(8,128)(2,1)} %moe_layer.1) | data formatting | bytes 524288

commit v2 on v1

--- a/solution.py
+++ b/solution.py
@@ -7,7 +7,7 @@
 from jax.experimental.pallas import tpu as pltpu
 from jax.sharding import PartitionSpec as P
 
-ORDER = (0, 1, 7, 2, 6, 3, 5, 4)
+ORDER = (4, 3, 5, 2, 6, 1, 7, 0)
 BF = jnp.bfloat16
 F32 = jnp.float32
 
@@ -15,8 +15,7 @@
 def kernel(
     tub_ref, emb_ref, gain_ref, routes_ref, codes_ref, win_ref, wdn_ref,
     out_ref,
-    tub, emb, embedded, gate, disp, recv1, send2, xs, w1, w2, stage, part, own, acc, stage3, half2, back, ret1,
-    send3, ret2,
+    tub, emb, embedded, gate, disp, recv1, send2, xs, w1, w2, stage, part, own, stage3, half2, back, ret,
     load_sem, wl_sem, ws_sem, wr_sem, fs_sem, fr_sem, as_sem, ar_sem, zs_sem, zr_sem, gs_sem, gr_sem,
     hs_sem, hr_sem, ps_sem, pr_sem, ys_sem, yr_sem, bs_sem, br_sem,
 ):
@@ -80,7 +79,7 @@
         ex = routes_ref[k : k + 1, :]
         rank = jnp.sum(hot[k] * count, axis=0, keepdims=True).astype(jnp.int32)
         d = ((ex >> 3) - z) & 7
-        place = jnp.where(d <= 4, jnp.maximum(2 * d - 1, 0), 16 - 2 * d)
+        place = jnp.where(d < 4, 7 - 2 * d, 2 * d - 8)
         kind = (ex >> 2) & 1
         j = ((ex & 3) - (x + kind * (y - x))) & 3
         block = ((kind + c) & 1) * 4 + j
@@ -101,10 +100,10 @@
         cp = copy(disp.at[b], recv1.at[b], as_sem.at[b], ar_sem.at[b], line(core, j, core))
         cp.start()
         a_copies.append(cp)
-    sends += a_copies
+        sends.append(cp)
 
     w_copies = {}
-    for b in (1, 5, 3, 7, 4, 2, 6):
+    for b in (2, 6, 1, 5, 3, 7, 4):
         j, other = b % 4, b // 4
         core = other + c - 2 * other * c
         k = core * 4 + ((x + core * (y - x)) + j) % 4
@@ -131,9 +130,9 @@
         cp.wait_recv()
     moved = jnp.dot(perm, recv1[...].reshape(384, 1024), preferred_element_type=F32).astype(BF).reshape(8, 48, 1024)
     send2[...] = moved
-    xs[0, 0, 0:48] = moved[0]
-    z_copies = [None]
-    for p in range(1, 8):
+    xs[0, 3, 48:96] = moved[7]
+    z_copies = []
+    for p in range(7):
         dst = xs.at[0, p // 2, pl.ds(p % 2 * 48, 48)]
         cp = copy(send2.at[p], dst, zs_sem.at[p], zr_sem.at[p], (r, (z + ORDER[p]) % 8))
         cp.start()
@@ -161,9 +160,10 @@
             w_copies[2 + 4 * other, m] = cp
 
     g_copies = {}
-    for g in range(4):
+
+    def gather(g):
         for p in (2 * g, 2 * g + 1):
-            if p:
+            if p < 7:
                 z_copies[p].wait_recv()
         for j in (1, 3):
             cp = copy(xs.at[0, g], xs.at[j, g], gs_sem.at[g, j], gr_sem.at[g, j], b_line(j))
@@ -180,16 +180,7 @@
             g_copies[g, 4 + i] = cp
             sends.append(cp)
 
-    for g in range(4):
-        forward(g)
-
-    for cp in w_own:
-        cp.wait()
-    for b in range(1, 8):
-        for m in (0, 1):
-            w_copies[b, m].wait_recv()
-
-    h_copies, p_copies, y_copies = {}, {}, [None]
+    h_copies, p_copies, y_copies = {}, {}, []
 
     def compute(g):
         g_copies[g, 4].wait_recv()
@@ -225,49 +216,54 @@
         p_copies[g, 1].wait_recv()
         total = own[g] + stage3[0, g].astype(F32) + stage3[1, g].astype(F32)
         total = total.astype(BF)
-        back[g] = total
-        if g == 0:
-            ret1[0] = total[0:48]
+        tiles = total.reshape(96, 8, 128)
+        back[g] = tiles
         for p in (2 * g, 2 * g + 1):
-            if p:
+            for b in range(8):
+                j, other = b % 4, b // 4
+                first = p % 2 * 48 + b * 6
+                if p == 7 and b == 0:
+                    ret[7] = tiles[first : first + 6]
+                    continue
+                rep, _ = line(c, 4 - j, other + c - 2 * other * c)
                 cp = copy(
-                    back.at[g, pl.ds(p % 2 * 48, 48)], ret1.at[p], bs_sem.at[p], br_sem.at[p],
-                    (r, (z + 8 - ORDER[p]) % 8),
+                    back.at[g, pl.ds(first, 6)], ret.at[b * 8 + p], bs_sem.at[b * 8 + p], br_sem.at[b * 8 + p],
+                    (rep, (z + 8 - ORDER[p]) % 8),
                 )
                 cp.start()
                 y_copies.append(cp)
                 sends.append(cp)
 
+    gather(0)
+    gather(1)
+    forward(0)
+    gather(2)
+    forward(1)
+    gather(3)
+    for cp in w_own:
+        cp.wait()
+    for b in range(1, 8):
+        for m in (0, 1):
+            w_copies[b, m].wait_recv()
     compute(0)
+    forward(2)
     compute(1)
     pass_on(0)
+    forward(3)
     compute(2)
+    pass_on(1)
     finish(0)
-    pass_on(1)
     compute(3)
+    pass_on(2)
     finish(1)
-    pass_on(2)
     pass_on(3)
     finish(2)
     finish(3)
 
-    for cp in y_copies[1:]:
-        cp.wait_recv()
-    moved = jnp.dot(perm, ret1[...].reshape(384, 1024), preferred_element_type=F32).astype(BF).reshape(8, 48, 1024)
-    send3[...] = moved
-    ret2[0] = moved[0]
-    last = []
-    for b in range(1, 8):
-        j, other = b % 4, b // 4
-        core = other + c - 2 * other * c
-        cp = copy(send3.at[b], ret2.at[b], acc.at[b], acc.at[8 + b], line(c, 4 - j, core))
-        cp.start()
-        last.append(cp)
-        sends.append(cp)
-    for cp in last:
+    for cp in y_copies:
         cp.wait_recv()
     combined = lax.dot_general(
-        gate[...], ret2[...].reshape(384, 1024), (((0,), (0,)), ((), ())), preferred_element_type=F32
+        gate[...], ret[...].reshape(384, 1024), (((0,), (0,)), ((), ())), preferred_element_type=F32
     )
     out_ref[...] = (embedded[...].astype(F32) + combined).astype(BF)
     for cp in sends:
@@ -298,13 +294,10 @@
             vmem((4, 1024, 128), BF),
             vmem((4, 4, 96, 1024), BF),
             vmem((4, 96, 1024), F32),
-            dma((16,)),
             vmem((2, 4, 96, 1024), BF),
             vmem((2, 4, 48, 1024), BF),
-            vmem((4, 96, 1024), BF),
-            vmem((8, 48, 1024), BF),
-            vmem((8, 48, 1024), BF),
-            vmem((8, 48, 1024), BF),
+            vmem((4, 96, 8, 128), BF),
+            vmem((64, 6, 8, 128), BF),
             dma((2,)),
             dma((2,)),
             dma((16,)),
@@ -323,8 +316,8 @@
             dma((4, 2)),
             dma((4, 2)),
             dma((4, 2)),
-            dma((8,)),
-            dma((8,)),
+            dma((64,)),
+            dma((64,)),
         ],
         compiler_params=pltpu.CompilerParams(
             collective_id=0, has_side_effects=True, vmem_limit_bytes=60 * 1024 * 1024

time: 101 us -> 82.8 us (0.82)
  Pallas kernels: 98.9 us -> 81 us
    pallas_call x1, Pallas kernels: 98.9 us -> 81 us  [on_device(): pl.pallas_call(kernel, out_shape=jax.ShapeDtypeStruct((128, 1024), BF), i...]
where the time goes in v2:
time: 82.8 us; the launch traced here: 82.7 us
  Pallas kernels  81 us (98%)
  local copies, waits for them, and re-layouts  1.67 us (2%)
    pallas_call x1, Pallas kernels, on_device(): pl.pallas_call(kernel, out_shape=jax.ShapeDtypeStruct((128, 1024), BF), i...  81 us
    unnamed x1, local copies, waits for them, and re-layouts  1.67 us

profile of v2, /device:TPU:1, one launch (start us, length us, event | category | flops | bytes accessed | tf_op | source)
XLA Modules:
  0.0 82.7 jit_solution(10541848488276126712)
XLA Ops:
  0.0 81.0 %moe_layer.1 = bf16[128,1024]{1,0:T(8,128)(2,1)} custom-call(bf16[128,1536]{1,0:T(8,128)(2,1)} %tub_ref.1, bf16[1536,1024]{1,0:T(8,128)(2,1)} %emb_ref.1, f32[1,1024]{1,0:T(1,128)} %bitcast.3, s32[2,128]{1,0:T(2,128)} %bitcast.4, s32[2,128]{1,0:T(2,128)} %bitcast.5, bf16[8,1024,128]{2,1,0:T(8,128)(2,1)} %win_ref.1, bf16[8,1024,128]{2,1,0:T(8,128)(2,1)} %wdn_ref.1), custom_call_target="tpu_custom_call" | custom-call | tf_op jit(solution)/shard_map/moe_layer/pallas_call | solution.py:278
  81.0 1.7 %copy.9 = bf16[128,1024]{1,0:T(8,128)(2,1)} copy(bf16[128,1024]{1,0:T(8,128)(2,1)} %moe_layer.1) | data formatting | bytes 524288

commit v3 on v2

v3 whole, which is shorter than its diff:
```python
import functools

import jax
import jax.numpy as jnp
from jax import lax
from jax.experimental import pallas as pl
from jax.experimental.pallas import tpu as pltpu
from jax.sharding import PartitionSpec as P

ORDER = (4, 3, 5, 2, 6, 1, 7, 0)
BF = jnp.bfloat16
F32 = jnp.float32


def kernel(
    tub_ref, emb_ref, gain_hbm, routes_hbm, codes_hbm, win_ref, wdn_ref,
    out_ref,
    routes_ref, codes_ref, gain_ref, tub, emb, embedded, gate, disp, recv1, send2, xs, w1, w2, stage, part, own, stage3, half2, back, ret,
    load_sem, wl_sem, ws_sem, wr_sem, fs_sem, fr_sem, as_sem, ar_sem, zs_sem, zr_sem, gs_sem, gr_sem,
    hs_sem, hr_sem, ps_sem, pr_sem, ys_sem, yr_sem, bs_sem, br_sem,
):
    r = lax.axis_index("rep")
    z = lax.axis_index("exp")
    c = r % 2
    x = (r // 2) % 4
    y = r // 8

    def at(px, py, core, pz=None):
        rep = ((py + 8) % 4 * 4 + (px + 8) % 4) * 2 + core
        return (rep, z if pz is None else pz)

    def line(kind, j, core):
        return at(x + (1 - kind) * j, y + kind * j, core)

    def copy(src, dst, ssem, rsem, dev):
        return pltpu.make_async_remote_copy(
            src_ref=src, dst_ref=dst, send_sem=ssem, recv_sem=rsem, device_id=dev, device_id_type=pl.DeviceIdType.MESH
        )

    def arrive(ref, sem):
        copy(ref, ref, as_sem, sem, line(c, 1, c)).wait_recv()

    def leave(ref, sem):
        copy(ref, ref, sem, ar_sem, line(c, 1, c)).wait_send()

    loads = [
        pltpu.make_async_copy(src, dst, load_sem.at[i])
        for i, (src, dst) in enumerate(((routes_hbm, routes_ref), (codes_hbm, codes_ref), (gain_hbm, gain_ref)))
    ]
    for i in range(3):
        part_k = pl.ds(i * 512, 512)
        loads.append(pltpu.make_async_copy(tub_ref.at[:, part_k], tub.at[:, part_k], load_sem.at[3 + 2 * i]))
        loads.append(pltpu.make_async_copy(emb_ref.at[part_k], emb.at[part_k], load_sem.at[4 + 2 * i]))
    for cp in loads:
        cp.start()

    barrier = pltpu.get_barrier_semaphore()
    peers = [line(kind, j, core) for kind in (0, 1) for j in (1, 2, 3) for core in (0, 1)]
    peers += [at(x, y, 1 - c)] + [(r, (z + d) % 8) for d in range(1, 8)]
    for dev in peers:
        pl.semaphore_signal(barrier, inc=1, device_id=dev, device_id_type=pl.DeviceIdType.MESH)

    own_k = c * 4 + x + c * (y - x)
    w_own = [
        pltpu.make_async_copy(win_ref.at[own_k], w1.at[:, 0:128], wl_sem.at[0]),
        pltpu.make_async_copy(wdn_ref.at[own_k], w2.at[:, 0:128], wl_sem.at[1]),
    ]
    for cp in w_own:
        cp.start()
    for cp in loads[:3]:
        cp.wait()
    experts = lax.broadcasted_iota(jnp.int32, (64, 128), 0)
    hot = [(experts == routes_ref[k : k + 1, :]).astype(F32) for k in (0, 1)]
    before = (
        lax.broadcasted_iota(jnp.int32, (128, 128), 0) < lax.broadcasted_iota(jnp.int32, (128, 128), 1)
    ).astype(F32).astype(BF)
    count = jnp.dot((hot[0] + hot[1]).astype(BF), before, preferred_element_type=F32)
    slots = lax.broadcasted_iota(jnp.int32, (384, 128), 0)
    picks = []
    for k in (0, 1):
        ex = routes_ref[k : k + 1, :]
        rank = jnp.sum(hot[k] * count, axis=0, keepdims=True).astype(jnp.int32)
        d = ((ex >> 3) - z) & 7
        place = jnp.where(d < 4, 7 - 2 * d, 2 * d - 8)
        kind = (ex >> 2) & 1
        j = ((ex & 3) - (x + kind * (y - x))) & 3
        block = ((kind + c) & 1) * 4 + j
        picks.append(slots == block * 48 + place * 6 + rank)
    dispatch = (picks[0].astype(F32) + picks[1].astype(F32)).astype(BF)
    vals = [0.25 + 0.125 * codes_ref[k : k + 1, :].astype(F32) for k in (0, 1)]
    gate[...] = (picks[0].astype(F32) * vals[0] + picks[1].astype(F32) * vals[1]).astype(BF)
    ri = lax.broadcasted_iota(jnp.int32, (384, 384), 0)
    ci = lax.broadcasted_iota(jnp.int32, (384, 384), 1)
    perm = (ci == (ri % 48) // 6 * 48 + ri // 48 * 6 + ri % 6).astype(F32).astype(BF)

    e = jnp.zeros((128, 1024), F32)
    for i in range(3):
        loads[3 + 2 * i].wait()
        loads[4 + 2 * i].wait()
        part_k = slice(i * 512, i * 512 + 512)
        e += jnp.dot(tub[:, part_k], emb[part_k, :], preferred_element_type=F32)
    e = e.astype(BF)
    embedded[...] = e
    ef = e.astype(F32)
    centred = ef - jnp.mean(ef, axis=-1, keepdims=True)
    var = jnp.mean(centred * centred, axis=-1, keepdims=True)
    normed = (centred * lax.rsqrt(var + 1e-06) * gain_ref[...]).astype(BF)

    rows = jnp.dot(dispatch, normed, preferred_element_type=F32).astype(BF).reshape(8, 48, 1024)
    disp[...] = rows
    recv1[0] = rows[0]
    pl.semaphore_wait(barrier, 20)

    for b in range(1, 8):
        j, other = b % 4, b // 4
        core = other + c - 2 * other * c
        cp = copy(disp.at[b], recv1.at[b], as_sem, ar_sem, line(core, j, core))
        cp.start()

    for b in (2, 6, 1, 5, 3, 7, 4):
        j, other = b % 4, b // 4
        core = other + c - 2 * other * c
        k = core * 4 + ((x + core * (y - x)) + j) % 4
        cols = pl.ds(b * 128, 128)
        for m, (src, dst) in enumerate(((win_ref, w1), (wdn_ref, w2))):
            if j == 2:
                step = 1 if m == 0 else 3
                cp = copy(
                    src.at[k], stage.at[m * 2 + other], ws_sem.at[m], fr_sem.at[m * 2 + other],
                    line(core, step, core),
                )
            else:
                cp = copy(
                    src.at[k], dst.at[:, cols], ws_sem.at[m], wr_sem.at[m], line(core, j, core)
                )
            cp.start()

    arrive(recv1.at[pl.ds(1, 7)], ar_sem)
    moved = jnp.dot(perm, recv1[...].reshape(384, 1024), preferred_element_type=F32).astype(BF).reshape(8, 48, 1024)
    send2[...] = moved
    xs[0, 3, 48:96] = moved[7]
    for p in range(7):
        dst = xs.at[0, p // 2, pl.ds(p % 2 * 48, 48)]
        cp = copy(send2.at[p], dst, zs_sem, zr_sem.at[p // 2], (r, (z + ORDER[p]) % 8))
        cp.start()

    def b_line(j):
        return line(1 - c, j, c)

    for m in (0, 1):
        for other in (0, 1):
            copy(
                win_ref.at[0], stage.at[m * 2 + other], fs_sem, fr_sem.at[m * 2 + other],
                line(c, 1, c),
            ).wait_recv()
            cols = pl.ds((2 + 4 * other) * 128, 128)
            cp = copy(
                stage.at[m * 2 + other], (w1, w2)[m].at[:, cols], fs_sem, wr_sem.at[m], line(c, 1 if m == 0 else 3, c),
            )
            cp.start()

    g_copies = {}

    def gather(g):
        arrive(xs.at[0, g] if g < 3 else xs.at[0, g, pl.ds(0, 48)], zr_sem.at[g])
        for j in (1, 3):
            cp = copy(xs.at[0, g], xs.at[j, g], gs_sem, gr_sem.at[g, j // 2], b_line(j))
            cp.start()
            g_copies[g, j] = cp

    def forward(g):
        for j, i in ((1, 0), (3, 1)):
            g_copies[g, j].wait_recv()
            half = pl.ds(i * 48, 48)
            cp = copy(xs.at[j, g, half], xs.at[2, g, half], hs_sem, hr_sem.at[g], b_line(j))
            cp.start()

    h_copies = {}

    def compute(g):
        arrive(xs.at[2, g], hr_sem.at[g])
        block = xs[:, g].reshape(384, 1024)
        hidden = jnp.dot(block, w1[...], preferred_element_type=F32)
        hidden = jax.nn.gelu(hidden).astype(BF)
        res = lax.dot_general(hidden, w2[...], (((1,), (1,)), ((), ())), preferred_element_type=F32)
        res = res.reshape(4, 96, 1024)
        own[g] = res[0]
        for j in (2, 1, 3):
            part[j, g] = res[j].astype(BF)
        for i, j in ((0, 3), (1, 1)):
            cp = copy(
                part.at[2, g, pl.ds(i * 48, 48)], half2.at[i, g], ps_sem, pr_sem.at[g, i], b_line(j)
            )
            cp.start()
            h_copies[g, i] = cp

    def pass_on(g):
        for i, j in ((0, 1), (1, 3)):
            h_copies[g, i].wait_recv()
            half = pl.ds(i * 48, 48)
            part[j, g, half] = (part[j, g, half].astype(F32) + half2[i, g].astype(F32)).astype(BF)
            cp = copy(part.at[j, g], stage3.at[j // 2, g], ys_sem, yr_sem.at[g], b_line(4 - j))
            cp.start()

    def finish(g):
        arrive(stage3.at[:, g], yr_sem.at[g])
        total = own[g] + stage3[0, g].astype(F32) + stage3[1, g].astype(F32)
        total = total.astype(BF)
        tiles = total.reshape(96, 8, 128)
        back[g] = tiles
        for p in (2 * g, 2 * g + 1):
            for b in range(8):
                j, other = b % 4, b // 4
                first = p % 2 * 48 + b * 6
                if p == 7 and b == 0:
                    ret[7] = tiles[first : first + 6]
                    continue
                rep, _ = line(c, 4 - j, other + c - 2 * other * c)
                cp = copy(
                    back.at[g, pl.ds(first, 6)], ret.at[b * 8 + p], bs_sem, br_sem,
                    (rep, (z + 8 - ORDER[p]) % 8),
                )
                cp.start()

    gather(0)
    gather(1)
    forward(0)
    gather(2)
    forward(1)
    gather(3)
    for cp in w_own:
        cp.wait()
    for m in (0, 1):
        arrive((w1, w2)[m].at[:, pl.ds(128, 896)], wr_sem.at[m])
    compute(0)
    forward(2)
    compute(1)
    pass_on(0)
    forward(3)
    compute(2)
    pass_on(1)
    finish(0)
    compute(3)
    pass_on(2)
    finish(1)
    pass_on(3)
    finish(2)
    finish(3)

    arrive(ret.at[pl.ds(0, 63)], br_sem)
    combined = lax.dot_general(
        gate[...], ret[...].reshape(384, 1024), (((0,), (0,)), ((), ())), preferred_element_type=F32
    )
    out_ref[...] = (embedded[...].astype(F32) + combined).astype(BF)
    leave(disp.at[pl.ds(1, 7)], as_sem)
    leave(win_ref.at[pl.ds(0, 7)], ws_sem.at[0])
    leave(wdn_ref.at[pl.ds(0, 7)], ws_sem.at[1])
    leave(stage, fs_sem)
    leave(send2.at[pl.ds(0, 7)], zs_sem)
    leave(xs.at[pl.ds(0, 2)], gs_sem)
    leave(xs.at[0], hs_sem)
    leave(part.at[2], ps_sem)
    leave(part.at[pl.ds(0, 2)], ys_sem)
    leave(ret.at[pl.ds(0, 63)], bs_sem)


def on_device(tubelets, embed_weight, norm_gain, routes, gate_codes, w_in, w_down):
    dma = pltpu.SemaphoreType.DMA
    vmem = pltpu.VMEM
    anyspace = pl.BlockSpec(memory_space=pl.ANY)
    local = pl.BlockSpec(memory_space=pltpu.VMEM)
    return pl.pallas_call(
        kernel,
        out_shape=vmem((128, 1024), BF),
        in_specs=[anyspace] * 7,
        out_specs=local,
        scratch_shapes=[
            vmem((2, 128), jnp.int32),
            vmem((2, 128), jnp.int32),
            vmem((1, 1024), F32),
            vmem((128, 1536), BF),
            vmem((1536, 1024), BF),
            vmem((128, 1024), BF),
            vmem((384, 128), BF),
            vmem((8, 48, 1024), BF),
            vmem((8, 48, 1024), BF),
            vmem((8, 48, 1024), BF),
            vmem((4, 4, 96, 1024), BF),
            vmem((1024, 1024), BF),
            vmem((1024, 1024), BF),
            vmem((4, 1024, 128), BF),
            vmem((4, 4, 96, 1024), BF),
            vmem((4, 96, 1024), F32),
            vmem((2, 4, 96, 1024), BF),
            vmem((2, 4, 48, 1024), BF),
            vmem((4, 96, 8, 128), BF),
            vmem((64, 6, 8, 128), BF),
            dma((9,)),
            dma((2,)),
            dma((2,)),
            dma((2,)),
            dma(()),
            dma((4,)),
            dma(()),
            dma(()),
            dma(()),
            dma((4,)),
            dma(()),
            dma((4, 2)),
            dma(()),
            dma((4,)),
            dma(()),
            dma((4, 2)),
            dma(()),
            dma((4,)),
            dma(()),
            dma(()),
        ],
        compiler_params=pltpu.CompilerParams(
            collective_id=0, has_side_effects=True, vmem_limit_bytes=60 * 1024 * 1024
        ),
        name="moe_layer",
    )(tubelets, embed_weight, norm_gain.reshape(1, 1024), routes.T, gate_codes.T, w_in, w_down)


def solution(mesh):
    return jax.shard_map(
        on_device,
        mesh=mesh,
        in_specs=(
            P(("rep", "exp"), None),
            P(),
            P(),
            P(("rep", "exp"), None),
            P(("rep", "exp"), None),
            P("exp", None, "rep"),
            P("exp", None, "rep"),
        ),
        out_specs=P(("rep", "exp"), None),
        check_vma=False,
    )
```

time: 82.8 us -> 78 us (0.942)
  Pallas kernels: 81 us -> 77.2 us
  local copies, waits for them, and re-layouts: 1.67 us -> 0.71 us
    pallas_call x1, Pallas kernels: 81 us -> 77.2 us  [on_device(): pl.pallas_call(kernel, out_shape=vmem((128, 1024), BF), in_specs=[anyspac...]
    unnamed x1, local copies, waits for them, and re-layouts: 1.67 us -> 0.71 us
where the time goes in v3:
time: 78 us; the launch traced here: 77.9 us
  Pallas kernels  77.2 us (99%)
    pallas_call x1, Pallas kernels, on_device(): pl.pallas_call(kernel, out_shape=vmem((128, 1024), BF), in_specs=[anyspac...  77.2 us

profile of v3, /device:TPU:1, one launch (start us, length us, event | category | flops | bytes accessed | tf_op | source)
XLA Modules:
  0.0 77.9 jit_solution(7914078934141772909)
XLA Ops:
  0.0 77.2 %moe_layer.1 = bf16[128,1024]{1,0:T(8,128)(2,1)S(1)} custom-call(bf16[128,1536]{1,0:T(8,128)(2,1)} %tub_ref.1, bf16[1536,1024]{1,0:T(8,128)(2,1)} %emb_ref.1, f32[1,1024]{1,0:T(1,128)} %bitcast.3, s32[2,128]{1,0:T(2,128)} %bitcast.4, s32[2,128]{1,0:T(2,128)} %bitcast.5, bf16[8,1024,128]{2,1,0:T(8,128)(2,1)} %win_ref.1, bf16[8,1024,128]{2,1,0:T(8,128)(2,1)} %wdn_ref.1), custom_call_target="tpu_custom_call" | custom-call | tf_op jit(solution)/shard_map/moe_layer/pallas_call | solution.py:272
  77.2 0.7 copy.9

commit v4 on v3

--- a/solution.py
+++ b/solution.py
@@ -8,6 +8,7 @@
 from jax.sharding import PartitionSpec as P
 
 ORDER = (4, 3, 5, 2, 6, 1, 7, 0)
+GROUPS = ((0, 1), (1, 2), (3, 2), (5, 2), (7, 1))
 BF = jnp.bfloat16
 F32 = jnp.float32
 
@@ -138,11 +139,11 @@
     arrive(recv1.at[pl.ds(1, 7)], ar_sem)
     moved = jnp.dot(perm, recv1[...].reshape(384, 1024), preferred_element_type=F32).astype(BF).reshape(8, 48, 1024)
     send2[...] = moved
-    xs[0, 3, 48:96] = moved[7]
-    for p in range(7):
-        dst = xs.at[0, p // 2, pl.ds(p % 2 * 48, 48)]
-        cp = copy(send2.at[p], dst, zs_sem, zr_sem.at[p // 2], (r, (z + ORDER[p]) % 8))
-        cp.start()
+    xs[0, 7] = moved[7]
+    for g, (first, places) in enumerate(GROUPS):
+        for p in range(first, min(first + places, 7)):
+            cp = copy(send2.at[p], xs.at[0, p], zs_sem, zr_sem.at[g], (r, (z + ORDER[p]) % 8))
+            cp.start()
 
     def b_line(j):
         return line(1 - c, j, c)
@@ -162,62 +163,71 @@
     g_copies = {}
 
     def gather(g):
-        arrive(xs.at[0, g] if g < 3 else xs.at[0, g, pl.ds(0, 48)], zr_sem.at[g])
+        first, places = GROUPS[g]
+        group = pl.ds(first, places)
+        if first < 7:
+            arrive(xs.at[0, pl.ds(first, min(places, 7 - first))], zr_sem.at[g])
         for j in (1, 3):
-            cp = copy(xs.at[0, g], xs.at[j, g], gs_sem, gr_sem.at[g, j // 2], b_line(j))
+            cp = copy(xs.at[0, group], xs.at[j, group], gs_sem, gr_sem.at[g, j // 2], b_line(j))
             cp.start()
             g_copies[g, j] = cp
 
     def forward(g):
+        group = pl.ds(*GROUPS[g])
         for j, i in ((1, 0), (3, 1)):
             g_copies[g, j].wait_recv()
-            half = pl.ds(i * 48, 48)
-            cp = copy(xs.at[j, g, half], xs.at[2, g, half], hs_sem, hr_sem.at[g], b_line(j))
+            half = pl.ds(i * 512, 512)
+            cp = copy(
+                xs.at[j, group, :, half], xs.at[2, group, :, half], hs_sem, hr_sem.at[g], b_line(j)
+            )
             cp.start()
 
     h_copies = {}
 
     def compute(g):
-        arrive(xs.at[2, g], hr_sem.at[g])
-        block = xs[:, g].reshape(384, 1024)
+        first, places = GROUPS[g]
+        group = pl.ds(first, places)
+        arrive(xs.at[2, group], hr_sem.at[g])
+        block = xs[:, group].reshape(4 * places * 48, 1024)
         hidden = jnp.dot(block, w1[...], preferred_element_type=F32)
         hidden = jax.nn.gelu(hidden).astype(BF)
         res = lax.dot_general(hidden, w2[...], (((1,), (1,)), ((), ())), preferred_element_type=F32)
-        res = res.reshape(4, 96, 1024)
-        own[g] = res[0]
+        res = res.reshape(4, places, 48, 1024)
+        own[group] = res[0]
         for j in (2, 1, 3):
-            part[j, g] = res[j].astype(BF)
+            part[j, group] = res[j].astype(BF)
         for i, j in ((0, 3), (1, 1)):
             cp = copy(
-                part.at[2, g, pl.ds(i * 48, 48)], half2.at[i, g], ps_sem, pr_sem.at[g, i], b_line(j)
+                part.at[2, group, :, pl.ds(i * 512, 512)], half2.at[i, group], ps_sem, pr_sem.at[g, i], b_line(j)
             )
             cp.start()
             h_copies[g, i] = cp
 
     def pass_on(g):
+        group = pl.ds(*GROUPS[g])
         for i, j in ((0, 1), (1, 3)):
             h_copies[g, i].wait_recv()
-            half = pl.ds(i * 48, 48)
-            part[j, g, half] = (part[j, g, half].astype(F32) + half2[i, g].astype(F32)).astype(BF)
-            cp = copy(part.at[j, g], stage3.at[j // 2, g], ys_sem, yr_sem.at[g], b_line(4 - j))
+            half = pl.ds(i * 512, 512)
+            part[j, group, :, half] = (part[j, group, :, half].astype(F32) + half2[i, group].astype(F32)).astype(BF)
+            cp = copy(part.at[j, group], stage3.at[j // 2, group], ys_sem, yr_sem.at[g], b_line(4 - j))
             cp.start()
 
     def finish(g):
-        arrive(stage3.at[:, g], yr_sem.at[g])
-        total = own[g] + stage3[0, g].astype(F32) + stage3[1, g].astype(F32)
-        total = total.astype(BF)
-        tiles = total.reshape(96, 8, 128)
-        back[g] = tiles
-        for p in (2 * g, 2 * g + 1):
+        first, places = GROUPS[g]
+        group = pl.ds(first, places)
+        arrive(stage3.at[:, group], yr_sem.at[g])
+        total = own[group] + stage3[0, group].astype(F32) + stage3[1, group].astype(F32)
+        tiles = total.astype(BF).reshape(places, 48, 8, 128)
+        back[group] = tiles
+        for p in range(first, first + places):
             for b in range(8):
                 j, other = b % 4, b // 4
-                first = p % 2 * 48 + b * 6
                 if p == 7 and b == 0:
-                    ret[7] = tiles[first : first + 6]
+                    ret[7] = tiles[p - first, 0:6]
                     continue
                 rep, _ = line(c, 4 - j, other + c - 2 * other * c)
                 cp = copy(
-                    back.at[g, pl.ds(first, 6)], ret.at[b * 8 + p], bs_sem, br_sem,
+                    back.at[p, pl.ds(b * 6, 6)], ret.at[b * 8 + p], bs_sem, br_sem,
                     (rep, (z + 8 - ORDER[p]) % 8),
                 )
                 cp.start()
@@ -228,24 +238,29 @@
     gather(2)
     forward(1)
     gather(3)
+    gather(4)
+    forward(2)
     for cp in w_own:
         cp.wait()
     for m in (0, 1):
         arrive((w1, w2)[m].at[:, pl.ds(128, 896)], wr_sem.at[m])
     compute(0)
-    forward(2)
     compute(1)
     pass_on(0)
     forward(3)
     compute(2)
     pass_on(1)
     finish(0)
+    forward(4)
     compute(3)
     pass_on(2)
     finish(1)
+    compute(4)
     pass_on(3)
     finish(2)
+    pass_on(4)
     finish(3)
+    finish(4)
 
     arrive(ret.at[pl.ds(0, 63)], br_sem)
     combined = lax.dot_general(
@@ -285,15 +300,15 @@
             vmem((8, 48, 1024), BF),
             vmem((8, 48, 1024), BF),
             vmem((8, 48, 1024), BF),
-            vmem((4, 4, 96, 1024), BF),
+            vmem((4, 8, 48, 1024), BF),
             vmem((1024, 1024), BF),
             vmem((1024, 1024), BF),
             vmem((4, 1024, 128), BF),
-            vmem((4, 4, 96, 1024), BF),
-            vmem((4, 96, 1024), F32),
-            vmem((2, 4, 96, 1024), BF),
-            vmem((2, 4, 48, 1024), BF),
-            vmem((4, 96, 8, 128), BF),
+            vmem((4, 8, 48, 1024), BF),
+            vmem((8, 48, 1024), F32),
+            vmem((2, 8, 48, 1024), BF),
+            vmem((2, 8, 48, 512), BF),
+            vmem((8, 48, 8, 128), BF),
             vmem((64, 6, 8, 128), BF),
             dma((9,)),
             dma((2,)),
@@ -304,15 +319,15 @@
             dma(()),
             dma(()),
             dma(()),
-            dma((4,)),
-            dma(()),
-            dma((4, 2)),
-            dma(()),
-            dma((4,)),
-            dma(()),
-            dma((4, 2)),
-            dma(()),
-            dma((4,)),
+            dma((len(GROUPS),)),
+            dma(()),
+            dma((len(GROUPS), 2)),
+            dma(()),
+            dma((len(GROUPS),)),
+            dma(()),
+            dma((len(GROUPS), 2)),
+            dma(()),
+            dma((len(GROUPS),)),
             dma(()),
             dma(()),
         ],

time: 78 us -> 76.5 us (0.981)
  Pallas kernels: 77.2 us -> 75.7 us
    pallas_call x1, Pallas kernels: 77.2 us -> 75.7 us  [on_device(): pl.pallas_call(kernel, out_shape=vmem((128, 1024), BF), in_specs=[anyspac...]
where the time goes in v4:
time: 76.5 us; the launch traced here: 76.4 us
  Pallas kernels  75.7 us (99%)
    pallas_call x1, Pallas kernels, on_device(): pl.pallas_call(kernel, out_shape=vmem((128, 1024), BF), in_specs=[anyspac...  75.7 us

profile of v4, /device:TPU:1, one launch (start us, length us, event | category | flops | bytes accessed | tf_op | source)
XLA Modules:
  0.0 76.4 jit_solution(16133436614630627878)
XLA Ops:
  0.0 75.7 %moe_layer.1 = bf16[128,1024]{1,0:T(8,128)(2,1)S(1)} custom-call(bf16[128,1536]{1,0:T(8,128)(2,1)} %tub_ref.1, bf16[1536,1024]{1,0:T(8,128)(2,1)} %emb_ref.1, f32[1,1024]{1,0:T(1,128)} %bitcast.3, s32[2,128]{1,0:T(2,128)} %bitcast.4, s32[2,128]{1,0:T(2,128)} %bitcast.5, bf16[8,1024,128]{2,1,0:T(8,128)(2,1)} %win_ref.1, bf16[8,1024,128]{2,1,0:T(8,128)(2,1)} %wdn_ref.1), custom_call_target="tpu_custom_call" | custom-call | tf_op jit(solution)/shard_map/moe_layer/pallas_call | solution.py:287
  75.7 0.7 copy.9

commit v5 on v4

--- a/solution.py
+++ b/solution.py
@@ -16,7 +16,7 @@
 def kernel(
     tub_ref, emb_ref, gain_hbm, routes_hbm, codes_hbm, win_ref, wdn_ref,
     out_ref,
-    routes_ref, codes_ref, gain_ref, tub, emb, embedded, gate, disp, recv1, send2, xs, w1, w2, stage, part, own, stage3, half2, back, ret,
+    routes_ref, codes_ref, gain_ref, tub, emb, embedded, gate, disp, recv1, send2, xs, w1, w2, stage, part, own, stage3, half2, far, back, ret,
     load_sem, wl_sem, ws_sem, wr_sem, fs_sem, fr_sem, as_sem, ar_sem, zs_sem, zr_sem, gs_sem, gr_sem,
     hs_sem, hr_sem, ps_sem, pr_sem, ys_sem, yr_sem, bs_sem, br_sem,
 ):
@@ -196,6 +196,11 @@
         own[group] = res[0]
         for j in (2, 1, 3):
             part[j, group] = res[j].astype(BF)
+        if g == 0:
+            copy(part.at[2, group], far, ps_sem, pr_sem.at[0, 0], b_line(2)).start()
+            for j in (1, 3):
+                copy(part.at[j, group], stage3.at[j // 2, group], ys_sem, yr_sem.at[0], b_line(4 - j)).start()
+            return
         for i, j in ((0, 3), (1, 1)):
             cp = copy(
                 part.at[2, group, :, pl.ds(i * 512, 512)], half2.at[i, group], ps_sem, pr_sem.at[g, i], b_line(j)
@@ -217,6 +222,9 @@
         group = pl.ds(first, places)
         arrive(stage3.at[:, group], yr_sem.at[g])
         total = own[group] + stage3[0, group].astype(F32) + stage3[1, group].astype(F32)
+        if g == 0:
+            arrive(far, pr_sem.at[0, 0])
+            total += far[...].astype(F32)
         tiles = total.astype(BF).reshape(places, 48, 8, 128)
         back[group] = tiles
         for p in range(first, first + places):
@@ -246,7 +254,6 @@
         arrive((w1, w2)[m].at[:, pl.ds(128, 896)], wr_sem.at[m])
     compute(0)
     compute(1)
-    pass_on(0)
     forward(3)
     compute(2)
     pass_on(1)
@@ -308,6 +315,7 @@
             vmem((8, 48, 1024), F32),
             vmem((2, 8, 48, 1024), BF),
             vmem((2, 8, 48, 512), BF),
+            vmem((1, 48, 1024), BF),
             vmem((8, 48, 8, 128), BF),
             vmem((64, 6, 8, 128), BF),
             dma((9,)),

time: 76.5 us -> 76.1 us (level)
  no operation moved by 1% of the time
where the time goes in v5:
time: 76.1 us; the launch traced here: 76 us
  Pallas kernels  75.3 us (99%)
    pallas_call x1, Pallas kernels, on_device(): pl.pallas_call(kernel, out_shape=vmem((128, 1024), BF), in_specs=[anyspac...  75.3 us

profile of v5, /device:TPU:1, one launch (start us, length us, event | category | flops | bytes accessed | tf_op | source)
XLA Modules:
  0.0 76.0 jit_solution(7012275248323119432)
XLA Ops:
  0.0 75.3 %moe_layer.1 = bf16[128,1024]{1,0:T(8,128)(2,1)S(1)} custom-call(bf16[128,1536]{1,0:T(8,128)(2,1)} %tub_ref.1, bf16[1536,1024]{1,0:T(8,128)(2,1)} %emb_ref.1, f32[1,1024]{1,0:T(1,128)} %bitcast.3, s32[2,128]{1,0:T(2,128)} %bitcast.4, s32[2,128]{1,0:T(2,128)} %bitcast.5, bf16[8,1024,128]{2,1,0:T(8,128)(2,1)} %win_ref.1, bf16[8,1024,128]{2,1,0:T(8,128)(2,1)} %wdn_ref.1), custom_call_target="tpu_custom_call" | custom-call | tf_op jit(solution)/shard_map/moe_layer/pallas_call | solution.py:294
  75.3 0.7 copy.9

commit v6 on v4

--- a/solution.py
+++ b/solution.py
@@ -16,7 +16,7 @@
 def kernel(
     tub_ref, emb_ref, gain_hbm, routes_hbm, codes_hbm, win_ref, wdn_ref,
     out_ref,
-    routes_ref, codes_ref, gain_ref, tub, emb, embedded, gate, disp, recv1, send2, xs, w1, w2, stage, part, own, stage3, half2, back, ret,
+    routes_ref, codes_ref, gain_ref, tub, emb, embedded, gate, disp, recv1, send2, xs, w1, w2, stage, part, own, stage3, half2, far, back, ret,
     load_sem, wl_sem, ws_sem, wr_sem, fs_sem, fr_sem, as_sem, ar_sem, zs_sem, zr_sem, gs_sem, gr_sem,
     hs_sem, hr_sem, ps_sem, pr_sem, ys_sem, yr_sem, bs_sem, br_sem,
 ):
@@ -196,6 +196,11 @@
         own[group] = res[0]
         for j in (2, 1, 3):
             part[j, group] = res[j].astype(BF)
+        if g in (0, 4):
+            copy(part.at[2, group], far.at[pl.ds(g // 4, 1)], ps_sem, pr_sem.at[g, 0], b_line(2)).start()
+            for j in (1, 3):
+                copy(part.at[j, group], stage3.at[j // 2, group], ys_sem, yr_sem.at[g], b_line(4 - j)).start()
+            return
         for i, j in ((0, 3), (1, 1)):
             cp = copy(
                 part.at[2, group, :, pl.ds(i * 512, 512)], half2.at[i, group], ps_sem, pr_sem.at[g, i], b_line(j)
@@ -217,6 +222,9 @@
         group = pl.ds(first, places)
         arrive(stage3.at[:, group], yr_sem.at[g])
         total = own[group] + stage3[0, group].astype(F32) + stage3[1, group].astype(F32)
+        if g in (0, 4):
+            arrive(far.at[pl.ds(g // 4, 1)], pr_sem.at[g, 0])
+            total += far[g // 4 : g // 4 + 1].astype(F32)
         tiles = total.astype(BF).reshape(places, 48, 8, 128)
         back[group] = tiles
         for p in range(first, first + places):
@@ -246,7 +254,6 @@
         arrive((w1, w2)[m].at[:, pl.ds(128, 896)], wr_sem.at[m])
     compute(0)
     compute(1)
-    pass_on(0)
     forward(3)
     compute(2)
     pass_on(1)
@@ -258,7 +265,6 @@
     compute(4)
     pass_on(3)
     finish(2)
-    pass_on(4)
     finish(3)
     finish(4)
 
@@ -308,6 +314,7 @@
             vmem((8, 48, 1024), F32),
             vmem((2, 8, 48, 1024), BF),
             vmem((2, 8, 48, 512), BF),
+            vmem((2, 48, 1024), BF),
             vmem((8, 48, 8, 128), BF),
             vmem((64, 6, 8, 128), BF),
             dma((9,)),

time: 76.5 us -> 76.3 us (level)
  no operation moved by 1% of the time
where the time goes in v6:
time: 76.3 us; the launch traced here: 76.2 us
  Pallas kernels  75.5 us (99%)
    pallas_call x1, Pallas kernels, on_device(): pl.pallas_call(kernel, out_shape=vmem((128, 1024), BF), in_specs=[anyspac...  75.5 us

profile of v6, /device:TPU:1, one launch (start us, length us, event | category | flops | bytes accessed | tf_op | source)
XLA Modules:
  0.0 76.2 jit_solution(1689981114584140942)
XLA Ops:
  0.0 75.5 %moe_layer.1 = bf16[128,1024]{1,0:T(8,128)(2,1)S(1)} custom-call(bf16[128,1536]{1,0:T(8,128)(2,1)} %tub_ref.1, bf16[1536,1024]{1,0:T(8,128)(2,1)} %emb_ref.1, f32[1,1024]{1,0:T(1,128)} %bitcast.3, s32[2,128]{1,0:T(2,128)} %bitcast.4, s32[2,128]{1,0:T(2,128)} %bitcast.5, bf16[8,1024,128]{2,1,0:T(8,128)(2,1)} %win_ref.1, bf16[8,1024,128]{2,1,0:T(8,128)(2,1)} %wdn_ref.1), custom_call_target="tpu_custom_call" | custom-call | tf_op jit(solution)/shard_map/moe_layer/pallas_call | solution.py:293
  75.5 0.7 copy.9
